TPU v7x, 512 devices: a whole 4x8x8 slice. The times are simulated.
512 devices in a mesh: sat: 16 (over z, core), seg: 32 (over y, x).
Axes of the slice: x: 4, y: 8, z: 8, core: 2. Of those that a mesh axis runs over, the one named last changes fastest.
Arguments:
- sens_params: bfloat16 [16, 32, 320, 1024], P('sat', 'seg'), may hold values from -0.59765625 to 0.59765625
- sens_state: bfloat16 [16, 32, 320, 64], P('sat', 'seg'), may hold values from -0.59765625 to 0.59765625
- misfit: float32 [16, 32, 320], P('sat', 'seg'), may hold values from -6 to 6
- depth: float32 [16, 32, 320], P('sat', 'seg'), may hold values from 0.2 to 0.9
- cycle_count: int32 [16, 32], P('sat', 'seg'), may hold values from 80 to 320, as said below
- node_side: int32 [16, 32, 320], P('sat', 'seg'), may hold values from 0 to 1, as said below
- transition: bfloat16 [16, 32, 64, 64], P('sat', 'seg'), may hold values from -0.75 to 0.75
- cont_sens: bfloat16 [16, 32, 64, 1024], P('sat', 'seg'), may hold values from -0.59765625 to 0.59765625
- noise_root: float32 [16, 32, 64, 64], P('sat', 'seg'), may hold values from -0.4 to 0.4
- cont_misfit: float32 [16, 32, 64], P('sat', 'seg'), may hold values from -6 to 6
Outputs:
- gram_params: float32 [1024, 1024], P('sat')
- grad_params: float32 [1024], replicated
- node_hess: float32 [16, 32, 64, 64], P('sat', 'seg')
- node_cross: float32 [16, 32, 64, 1024], P('sat', 'seg')
- node_grad: float32 [16, 32, 64], P('sat', 'seg')
- node_coupling: float32 [16, 32, 64, 64], P('sat', 'seg')
Inputs may be any that keep to these rules, and one draw needn't show every extreme that they name: `cycle_count`: in every segment some satellite has exactly 320 cycles. `node_side`: along the cycles of one satellite's segment the value never falls, and both values occur.
All inputs are finite; a program needn't handle non-finite values.
Results may differ from a plain program's by a relative error of at most 0.0015.
The roundings to bfloat16 on the way count: a program that leaves them out, or rounds other values in their place, can miss the bound.
Values sent between devices are 32-bit elements; how exact they have to be, the bound alone decides.
A program may use at most 64 MiB of HBM per device.

v0:
```python
import jax
import jax.numpy as jnp
from jax import lax
from jax.sharding import PartitionSpec as P

highest = lax.Precision.HIGHEST


def entering(value, axis, combine, identity):
    devices, position = (lax.axis_size(axis), lax.axis_index(axis))
    everything = lax.all_gather(value, axis)
    start = jnp.broadcast_to(jnp.asarray(identity, value.dtype), value.shape)

    def step(k, before):
        reached = k < position
        new = combine(before, everything[k])
        return jnp.where(reached, new, before)

    return lax.fori_loop(0, devices, step, start)


def passed_along(block, axis, distance):
    devices = range(lax.axis_size(axis))
    route = [(i - distance, i) for i in devices if i - distance in devices]
    return lax.ppermute(block, axis, route)


def add_pair(earlier, later):
    return earlier + later


def shards(
    sens_params,
    sens_state,
    misfit,
    depth,
    cycle_count,
    node_side,
    transition,
    cont_sens,
    noise_root,
    cont_misfit,
):
    sat_dev = sens_params.shape[0]
    cycles = sens_params.shape[2]
    params = sens_params.shape[3]
    states = sens_state.shape[3]
    sat_count = lax.axis_size("sat")
    seg_count = lax.axis_size("seg")
    seg_place = lax.axis_index("seg")
    positions = jnp.arange(cycles, dtype=jnp.int32)
    live_mask = (positions[None, :] < cycle_count).astype(jnp.float32)
    used_depth = live_mask * depth[:, 0]
    through = jnp.sum(used_depth, axis=1)
    prior_age = entering(through, "seg", add_pair, jnp.zeros_like(through))
    upper_tri = (positions[:, None] < positions[None, :]).astype(jnp.float32)
    inner_age = jnp.dot(used_depth, upper_tri, precision=highest)
    age_scale = 4.0 / (cycles * seg_count)
    weights = live_mask / (1.0 + (prior_age[:, None] + inner_age) * age_scale)
    root_seg = jnp.sqrt(weights)
    weighted_sens = (root_seg[:, :, None] * sens_params[:, 0]).astype(jnp.bfloat16)
    weighted_res = (root_seg * misfit[:, 0]).astype(jnp.bfloat16)
    side = node_side[:, 0].astype(jnp.float32)[:, :, None]
    state_rows = root_seg[:, :, None] * sens_state[:, 0]
    state_pair = jnp.concatenate([state_rows * (1.0 - side), state_rows * side], axis=2).astype(
        jnp.bfloat16
    )
    live_link = (seg_place < seg_count - 1).astype(jnp.float32)
    eye_block = jnp.eye(states, dtype=jnp.float32)
    root_info = (eye_block[None] + noise_root[:, 0]) * live_link
    state_map = jnp.einsum(
        "sab,sbc->sac", root_info, transition[:, 0].astype(jnp.float32), precision=highest
    )
    param_map = jnp.einsum(
        "sab,sbp->sap", root_info, cont_sens[:, 0].astype(jnp.float32), precision=highest
    ).astype(jnp.bfloat16)
    cont_res = jnp.einsum("sab,sb->sa", root_info, cont_misfit[:, 0], precision=highest).astype(
        jnp.bfloat16
    )
    stacked = jnp.concatenate([weighted_sens, param_map], axis=1).reshape(-1, params)
    res_vec = jnp.concatenate([weighted_res, -cont_res], axis=1).reshape(-1)
    norm_factor = 1.0 / (sat_dev * sat_count * seg_count)
    term = lax.dot_general(
        stacked, stacked, (((0,), (0,)), ((), ())), preferred_element_type=jnp.float32
    )
    row_block = lax.psum_scatter(
        term * norm_factor, ("sat", "seg"), scatter_dimension=0, tiled=True
    )
    gram_params = lax.all_gather(row_block, "seg", axis=0, tiled=True)
    grad_term = jnp.dot(res_vec, stacked, preferred_element_type=jnp.float32) * norm_factor
    grad_params = lax.psum(grad_term, ("sat", "seg"))
    pair_gram = jnp.einsum(
        "smi,smk->sik", state_pair, state_pair, preferred_element_type=jnp.float32
    )
    pair_cross = jnp.einsum(
        "smi,smp->sip", state_pair, weighted_sens, preferred_element_type=jnp.float32
    )
    pair_grad = jnp.einsum(
        "smi,sm->si", state_pair, weighted_res, preferred_element_type=jnp.float32
    )
    map_float = param_map.astype(jnp.float32)
    res_float = cont_res.astype(jnp.float32)
    own_hess = pair_gram[:, :states, :states] + jnp.einsum(
        "sai,saj->sij", state_map, state_map, precision=highest
    )
    own_cross = pair_cross[:, :states] + jnp.einsum(
        "sai,sap->sip", state_map, map_float, precision=highest
    )
    own_grad = pair_grad[:, :states] - jnp.einsum(
        "sai,sa->si", state_map, res_float, precision=highest
    )
    next_hess = pair_gram[:, states:, states:] + jnp.einsum(
        "sai,saj->sij", root_info, root_info, precision=highest
    )
    next_cross = pair_cross[:, states:] - jnp.einsum(
        "sai,sap->sip", root_info, map_float, precision=highest
    )
    next_grad = pair_grad[:, states:] + jnp.einsum(
        "sai,sa->si", root_info, res_float, precision=highest
    )
    coupling = -jnp.einsum("sai,saj->sij", state_map, root_info, precision=highest)
    got_hess, got_cross, got_grad = passed_along((next_hess, next_cross, next_grad), "seg", 1)
    node_hess = (own_hess + got_hess)[:, None]
    node_cross = (own_cross + got_cross)[:, None]
    node_grad = (own_grad + got_grad)[:, None]
    node_coupling = coupling[:, None]
    return (gram_params, grad_params, node_hess, node_cross, node_grad, node_coupling)


def solution(mesh):
    placed = (
        P("sat", "seg", None, None),
        P("sat", "seg", None, None),
        P("sat", "seg", None),
        P("sat", "seg", None),
        P("sat", "seg"),
        P("sat", "seg", None),
        P("sat", "seg", None, None),
        P("sat", "seg", None, None),
        P("sat", "seg", None, None),
        P("sat", "seg", None),
    )
    return jax.shard_map(
        shards,
        mesh=mesh,
        in_specs=placed,
        out_specs=(
            P("sat", None),
            P(),
            P("sat", "seg", None, None),
            P("sat", "seg", None, None),
            P("sat", "seg", None),
            P("sat", "seg", None, None),
        ),
        check_vma=False,
    )
```

profile of v0, /device:TPU:16, one launch (start us, length us, event | category | flops | bytes accessed | tf_op | source)
XLA Modules:
  0.0 479.6 jit_solution(1217586959932746977)
XLA Ops:
  7.9 1.3 fusion.38
  9.2 1.3 dynamic-slice
  10.5 1.4 dynamic-update-slice
  11.9 63.0 %all-reduce = f32[32]{0:T(128)S(1)} all-reduce(f32[32]{0:T(128)S(1)} %dynamic-update-slice), channel_id=1, replica_groups=mesh['sat'=16,'seg'=32] {'seg'}, use_global_device_ids=true, to_apply=%add | all-reduce | flops 32 | bytes 256
  74.8 40.4 %while.13 = (s32[]{:T(128)}, f32[1]{0:T(128)}, s32[]{:T(128)}, f32[32,1]{0,1:T(1,128)S(1)}, s32[]{:T(128)}) while((s32[]{:T(128)}, f32[1]{0:T(128)}, s32[]{:T(128)}, f32[32,1]{0,1:T(1,128)S(1)}, s32[]{:T(128)}) %tuple.40), condition=%wide.region_2.3_spmd, body=%wide.region_1.2_spmd.sunk | while | flops 5 | bytes 115 | solution.py:19
  76.1 0.6 constant_dynamic-slice_fusion.2
  77.3 0.6 constant_dynamic-slice_fusion.2
  78.6 0.6 constant_dynamic-slice_fusion.2
  79.9 0.6 constant_dynamic-slice_fusion.2
  81.1 0.6 constant_dynamic-slice_fusion.2
  82.4 0.6 constant_dynamic-slice_fusion.2
  84.9 0.6 constant_dynamic-slice_fusion.2
  86.2 0.6 constant_dynamic-slice_fusion.2
  87.5 0.6 constant_dynamic-slice_fusion.2
  115.2 0.7 convert_reduce_fusion
  115.9 0.7 reduce.1
  116.6 0.7 reduce.3
  117.6 1.3 fusion.1
  119.2 3.3 convolution_multiply_fusion
  122.4 0.6 copy-done.5
  123.5 3.7 collective-permute-start.2
  127.6 3.1 collective-permute-start
  131.5 4.6 collective-permute-start.1
  136.5 0.9 fusion.8
  137.3 110.4 %psum.7 = f32[1024]{0:T(1024)} all-reduce(f32[1024]{0:T(1024)S(1)} %broadcast_multiply_fusion), channel_id=1, replica_groups=mesh['sat'=16,'seg'=32] {'sat','seg'}, use_global_device_ids=true, to_apply=%region_4.5 | all-reduce | flops 1024 | bytes 8192 | tf_op jit(solution)/shard_map/psum | solution.py:91
  247.8 0.7 fusion.15
  248.4 0.9 fusion.11
  249.3 1.0 fusion.6
  250.3 171.4 %all-reduce.4.cloned.1.call-done = f32[1024,1024]{1,0:T(8,128)} async-done(((f32[1024,1024]{1,0:T(8,128)}), f32[1024,1024]{1,0:T(8,128)}) %all-reduce.4.cloned.1.call-update) | async-done | bytes 4194320
  421.8 0.8 dynamic-slice_bitcast_fusion
  422.5 49.4 %all-gather = f32[32,2,1024]{2,1,0:T(2,128)S(1)} all-gather(f32[1,2,1024]{2,1,0:T(2,128)S(1)} %dynamic-slice_bitcast_fusion), channel_id=1, replica_groups=mesh['sat'=16,'seg'=32] {'seg'}, dimensions={0}, use_global_device_ids=true | all-gather | bytes 270336 | tf_op jit(solution)/shard_map/all_gather | solution.py:89
  471.9 0.9 reshape.312
  (59 shorter events, 16.0 us)
Async XLA Ops:
  7.2 111.7 %copy-start = (bf16[1,1,64,1024]{3,2,1,0:T(8,128)(2,1)S(1)}, bf16[1,1,64,1024]{3,2,1,0:T(8,128)(2,1)}, u32[]{:S(2)}) copy-start(bf16[1,1,64,1024]{3,2,1,0:T(8,128)(2,1)} %param.19) | copy-start | bytes 393220
  7.2 111.7 %copy-start.2 = (f32[1,1,64,64]{3,2,1,0:T(8,128)S(1)}, f32[1,1,64,64]{3,2,1,0:T(8,128)}, u32[]{:S(2)}) copy-start(f32[1,1,64,64]{3,2,1,0:T(8,128)} %param.20) | copy-start | bytes 49156
  7.2 414.6 %all-reduce.4.cloned.1.call-start = ((), (), s32[]{:S(2)}) async-start(), calls=%async_computation | async-start | bytes 8388608
  122.4 0.7 copy-start.5
  122.4 0.8 copy-start.3
  122.4 8.4 %copy-start.1 = (bf16[1,1,320,1024]{3,2,1,0:T(8,128)(2,1)S(1)}, bf16[1,1,320,1024]{3,2,1,0:T(8,128)(2,1)}, u32[]{:S(2)}) copy-start(bf16[1,1,320,1024]{3,2,1,0:T(8,128)(2,1)} %param.12) | copy-start | bytes 1966084
  123.5 124.3 %collective-permute-start.2 = (f32[1,64]{1,0:T(1,128)S(1)}, f32[1,64]{1,0:T(1,128)S(1)}, u32[]{:S(2)}, u32[]{:S(2)}) collective-permute-start(f32[1,64]{1,0:T(1,128)S(1)} %convolution_add_fusion), channel_id=1, source_target_pairs={{0,1},{1,2},{2,3},{3,4},{4,5},{5,6},{6,7},{7,8},{8,9},{9,10},{10,1... | collective-permute-start | bytes 776 | tf_op jit(solution)/shard_map/ppermute | solution.py:25
  127.6 8.7 %copy-start.4 = (bf16[1,1,64,64]{3,2,1,0:T(8,128)(2,1)S(1)}, bf16[1,1,64,64]{3,2,1,0:T(8,128)(2,1)}, u32[]{:S(2)}) copy-start(bf16[1,1,64,64]{3,2,1,0:T(8,128)(2,1)} %param.18) | copy-start | bytes 24580
  127.6 120.8 %collective-permute-start = (f32[1,64,64]{2,1,0:T(8,128)S(1)}, f32[1,64,64]{2,1,0:T(8,128)S(1)}, u32[]{:S(2)}, u32[]{:S(2)}) collective-permute-start(f32[1,64,64]{2,1,0:T(8,128)S(1)} %fusion.12), channel_id=1, source_target_pairs={{0,1},{1,2},{2,3},{3,4},{4,5},{5,6},{6,7},{7,8},{8,9},{9,10},{10,1... | collective-permute-start | bytes 49160 | tf_op jit(solution)/shard_map/ppermute | solution.py:25
  131.5 117.8 %collective-permute-start.1 = (f32[1,64,1024]{2,1,0:T(8,128)S(1)}, f32[1,64,1024]{2,1,0:T(8,128)S(1)}, u32[]{:S(2)}, u32[]{:S(2)}) collective-permute-start(f32[1,64,1024]{2,1,0:T(8,128)S(1)} %fusion.7), channel_id=1, source_target_pairs={{0,1},{1,2},{2,3},{3,4},{4,5},{5,6},{6,7},{7,8},{8,9},{9,10},{10,1... | collective-permute-start | bytes 786440 | tf_op jit(solution)/shard_map/ppermute | solution.py:25
Sparse Core Ops, SparseCore 0:
  122.6 299.1 all-reduce.3
where the time goes:
time: 481 us; the launch traced here: 480 us
  blocking collectives  223 us (46%)
  waiting for transfers between devices  171 us (36%)
  local copies, waits for them, and re-layouts  23.7 us (5%)
  loops' own time  21.7 us (5%)
  between operations  14.9 us (3%)
  starting transfers between devices  11.4 us (2%)
  matrix products  9.03 us (2%)
    unnamed x2, waiting for transfers between devices  171 us
    psum x1, blocking collectives, shards(): grad_params = lax.psum(grad_term, ('sat', 'seg'))  110 us
    unnamed x1, blocking collectives  63 us
    all_gather x1, blocking collectives, shards(): gram_params = lax.all_gather(row_block, 'seg', axis=0, tiled=True)  49.4 us
    another operation x1, loops' own time, entering(): return lax.fori_loop(0, devices, step, start)  21.7 us
    dynamic_slice x32, local copies, waits for them, and re-layouts, step(): new = combine(before, everything[k])  18.7 us
    ppermute x3, starting transfers between devices, passed_along(): return lax.ppermute(block, axis, route)  11.3 us
  transfers between devices with their start and end apart: 4, of which 1 were waited for; matrix products, arithmetic and copies ran while one was open for 1% of the time, Pallas kernels for 0%

commit v1 on v0

--- a/solution.py
+++ b/solution.py
@@ -86,7 +86,9 @@
     row_block = lax.psum_scatter(
         term * norm_factor, ("sat", "seg"), scatter_dimension=0, tiled=True
     )
-    gram_params = lax.all_gather(row_block, "seg", axis=0, tiled=True)
+    gram_params = jnp.concatenate(
+        lax.all_to_all(jnp.stack([row_block] * lax.axis_size("seg")), "seg", 0, 0), axis=0
+    )
     grad_term = jnp.dot(res_vec, stacked, preferred_element_type=jnp.float32) * norm_factor
     grad_params = lax.psum(grad_term, ("sat", "seg"))
     pair_gram = jnp.einsum(

time: 481 us -> 542 us (1.13)
  the two profiles are of different devices: /device:TPU:16 before, /device:TPU:1 now
where the time goes in v1:
time: 542 us; the launch traced here: 540 us
  waiting for transfers between devices  293 us (54%)
  blocking collectives  161 us (30%)
  local copies, waits for them, and re-layouts  24.6 us (5%)
  loops' own time  21.7 us (4%)
  between operations  14.9 us (3%)
  starting transfers between devices  10.9 us (2%)
  matrix products  9.05 us (2%)
    unnamed x2, waiting for transfers between devices  293 us
    psum x1, blocking collectives, shards(): grad_params = lax.psum(grad_term, ('sat', 'seg'))  99.3 us
    unnamed x1, blocking collectives  61.9 us
    another operation x1, loops' own time, entering(): return lax.fori_loop(0, devices, step, start)  21.7 us
    dynamic_slice x32, local copies, waits for them, and re-layouts, step(): new = combine(before, everything[k])  18.7 us
  transfers between devices with their start and end apart: 5, of which 1 were waited for; matrix products, arithmetic and copies ran while one was open for 1% of the time, Pallas kernels for 0%

profile of v1, /device:TPU:1, one launch (start us, length us, event | category | flops | bytes accessed | tf_op | source)
XLA Modules:
  0.0 540.4 jit_solution(5669127004442280263)
XLA Ops:
  7.9 1.3 fusion.38
  9.2 1.3 dynamic-slice
  10.5 1.4 dynamic-update-slice
  11.9 61.9 %all-reduce = f32[32]{0:T(128)S(1)} all-reduce(f32[32]{0:T(128)S(1)} %dynamic-update-slice), channel_id=1, replica_groups=mesh['sat'=16,'seg'=32] {'seg'}, use_global_device_ids=true, to_apply=%add | all-reduce | flops 32 | bytes 256
  73.8 40.4 %while.13 = (s32[]{:T(128)}, f32[1]{0:T(128)}, s32[]{:T(128)}, f32[32,1]{0,1:T(1,128)S(1)}, s32[]{:T(128)}) while((s32[]{:T(128)}, f32[1]{0:T(128)}, s32[]{:T(128)}, f32[32,1]{0,1:T(1,128)S(1)}, s32[]{:T(128)}) %tuple.40), condition=%wide.region_2.3_spmd, body=%wide.region_1.2_spmd.sunk | while | flops 5 | bytes 115 | solution.py:19
  75.0 0.6 constant_dynamic-slice_fusion.3
  76.3 0.6 constant_dynamic-slice_fusion.3
  77.5 0.6 constant_dynamic-slice_fusion.3
  78.8 0.6 constant_dynamic-slice_fusion.3
  80.1 0.6 constant_dynamic-slice_fusion.3
  81.3 0.6 constant_dynamic-slice_fusion.3
  82.6 0.6 constant_dynamic-slice_fusion.3
  85.1 0.6 constant_dynamic-slice_fusion.3
  114.2 0.7 convert_reduce_fusion
  114.9 0.7 reduce.1
  115.6 0.7 reduce.3
  116.5 1.3 fusion.1
  118.1 3.3 convolution_multiply_fusion
  121.4 0.8 copy-done.3
  122.6 1.3 collective-permute-start.2
  124.4 1.3 collective-permute-start
  126.4 1.3 collective-permute-start.1
  128.2 293.4 %all-reduce.4.cloned.1.call-done = f32[1024,1024]{1,0:T(8,128)} async-done(((f32[1024,1024]{1,0:T(8,128)}), f32[1024,1024]{1,0:T(8,128)}) %all-reduce.4.cloned.1.call-update) | async-done | bytes 4194320
  421.6 0.8 constant_dynamic-slice_fusion.1
  422.4 0.8 stack.2
  423.1 6.9 %all-to-all-start = ((f32[32,2,1024]{2,1,0:T(2,128)}), f32[32,2,1024]{2,1,0:T(2,128)S(1)}, u32[]{:S(2)}, u32[]{:S(2)}) async-start(f32[32,2,1024]{2,1,0:T(2,128)} %stack.2), calls=%async_computation | async-start | bytes 524288 | tf_op jit(solution)/shard_map/all_to_all | solution.py:90
  430.0 0.9 fusion.8
  430.9 99.3 %psum.7 = f32[1024]{0:T(1024)} all-reduce(f32[1024]{0:T(1024)S(1)} %broadcast_multiply_fusion), channel_id=1, replica_groups=mesh['sat'=16,'seg'=32] {'sat','seg'}, use_global_device_ids=true, to_apply=%region_4.5 | all-reduce | flops 1024 | bytes 8192 | tf_op jit(solution)/shard_map/psum | solution.py:93
  530.2 0.7 fusion.15
  530.8 0.9 fusion.11
  531.7 1.0 fusion.6
  532.7 0.9 reshape.307
  (61 shorter events, 16.6 us)
Async XLA Ops:
  7.2 110.6 %copy-start = (bf16[1,1,64,1024]{3,2,1,0:T(8,128)(2,1)S(1)}, bf16[1,1,64,1024]{3,2,1,0:T(8,128)(2,1)}, u32[]{:S(2)}) copy-start(bf16[1,1,64,1024]{3,2,1,0:T(8,128)(2,1)} %param.19) | copy-start | bytes 393220
  7.2 110.6 %copy-start.2 = (f32[1,1,64,64]{3,2,1,0:T(8,128)S(1)}, f32[1,1,64,64]{3,2,1,0:T(8,128)}, u32[]{:S(2)}) copy-start(f32[1,1,64,64]{3,2,1,0:T(8,128)} %param.20) | copy-start | bytes 49156
  7.2 414.4 %all-reduce.4.cloned.1.call-start = ((), (), s32[]{:S(2)}) async-start(), calls=%async_computation.1 | async-start | bytes 8388608
  121.3 0.8 copy-start.3
  121.3 1.0 copy-start.5
  121.3 4.3 copy-start.1
  122.6 407.6 %collective-permute-start.2 = (f32[1,64]{1,0:T(1,128)S(1)}, f32[1,64]{1,0:T(1,128)S(1)}, u32[]{:S(2)}, u32[]{:S(2)}) collective-permute-start(f32[1,64]{1,0:T(1,128)S(1)} %convolution_add_fusion), channel_id=1, source_target_pairs={{0,1},{1,2},{2,3},{3,4},{4,5},{5,6},{6,7},{7,8},{8,9},{9,10},{10,1... | collective-permute-start | bytes 776 | tf_op jit(solution)/shard_map/ppermute | solution.py:25
  124.4 3.7 copy-start.4
  124.4 406.4 %collective-permute-start = (f32[1,64,64]{2,1,0:T(8,128)S(1)}, f32[1,64,64]{2,1,0:T(8,128)S(1)}, u32[]{:S(2)}, u32[]{:S(2)}) collective-permute-start(f32[1,64,64]{2,1,0:T(8,128)S(1)} %fusion.12), channel_id=1, source_target_pairs={{0,1},{1,2},{2,3},{3,4},{4,5},{5,6},{6,7},{7,8},{8,9},{9,10},{10,1... | collective-permute-start | bytes 49160 | tf_op jit(solution)/shard_map/ppermute | solution.py:25
  126.4 405.3 %collective-permute-start.1 = (f32[1,64,1024]{2,1,0:T(8,128)S(1)}, f32[1,64,1024]{2,1,0:T(8,128)S(1)}, u32[]{:S(2)}, u32[]{:S(2)}) collective-permute-start(f32[1,64,1024]{2,1,0:T(8,128)S(1)} %fusion.7), channel_id=1, source_target_pairs={{0,1},{1,2},{2,3},{3,4},{4,5},{5,6},{6,7},{7,8},{8,9},{9,10},{10,1... | collective-permute-start | bytes 786440 | tf_op jit(solution)/shard_map/ppermute | solution.py:25
  423.1 109.6 %all-to-all-start = ((f32[32,2,1024]{2,1,0:T(2,128)}), f32[32,2,1024]{2,1,0:T(2,128)S(1)}, u32[]{:S(2)}, u32[]{:S(2)}) async-start(f32[32,2,1024]{2,1,0:T(2,128)} %stack.2), calls=%async_computation | async-start | bytes 524288 | tf_op jit(solution)/shard_map/all_to_all | solution.py:90
Sparse Core Ops, SparseCore 0:
  121.5 300.0 all-reduce.3
